TPU v7x, 32 devices: a whole 2x2x4 slice. The times are simulated.
32 devices in a mesh: exp: 8 (over y, x, core), tp: 4 (over z).
Axes of the slice: x: 2, y: 2, z: 4, core: 2. Of those that a mesh axis runs over, the one named last changes fastest.
Arguments:
- tokens: bfloat16 [65536, 384], P(('exp', 'tp')), may hold values from -24 to 24
- cotangent: bfloat16 [65536, 384], P(('exp', 'tp')), may hold values from -1 to 1
- routes: int32 [65536, 2], P(('exp', 'tp')), may hold values from 0 to 7, all different within a row; in each aligned block of 2048 rows (0 to 2047, 2048 to 4095, ...) at most 1024 rows name the same one
- segments: int32 [64, 1024], P(('exp', 'tp')), may hold values from 0 to 7, never falling along the last dimension, each value on 1 to 256 neighbouring positions
- variates: int32 [64, 1024], P(('exp', 'tp')), may hold values from 0 to 3
- positions: int32 [64, 1024], P(('exp', 'tp')), may hold values from 0 to 1023
- step_count: int32 [1], replicated, may hold values from 1 to 20
- dense_state: float32 [4, 592896], P(None, ('exp', 'tp')), as said below
- gate_up_state: float32 [4, 8, 2, 384, 512], P(None, 'exp', None, None, 'tp'), as said below
- down_state: float32 [4, 8, 512, 384], P(None, 'exp', 'tp'), as said below
- small_state: float32 [4, 780], replicated, as said below
Outputs:
- block_out: bfloat16 [65536, 384], P(('exp', 'tp'))
- grad_in: bfloat16 [65536, 384], P(('exp', 'tp'))
- dense_new: float32 [4, 592896], P(None, ('exp', 'tp'))
- dense_copy: bfloat16 [592896], P(('exp', 'tp'))
- gate_up_new: float32 [4, 8, 2, 384, 512], P(None, 'exp', None, None, 'tp')
- gate_up_copy: bfloat16 [8, 2, 384, 512], P('exp', None, None, 'tp')
- down_new: float32 [4, 8, 512, 384], P(None, 'exp', 'tp')
- down_copy: bfloat16 [8, 512, 384], P('exp', 'tp')
- small_new: float32 [4, 780], replicated
Inputs may be any that keep to these rules, and one draw needn't show every extreme that they name: `routes`: in each aligned block of 2048 rows (the tokens of one device) no expert is named by more than 1024 rows, a bound that some block reaches; the 2 ids of a row differ. `segments`: within a row the ids never fall; a segment has at most a quarter of 1024 tokens. `dense_state`: index 2 is positive. `gate_up_state`: index 2 is positive. `down_state`: index 2 is positive. `small_state`: index 2 is positive.
All inputs are finite; a program needn't handle non-finite values.
Results may differ from a plain program's by a relative error of at most 0.015.
Values may be sent and summed in bfloat16 or wider, within the bound.
No kernel may reach another device: no remote copies, remote signals or barrier semaphores. Data moves between devices by JAX's collectives and lax.ppermute only.
A program may use at most 384 MiB of HBM per device.

v0:
```python
from functools import partial
import math
import jax
import jax.numpy as jnp
from jax import lax
from jax.sharding import PartitionSpec as P

D = 384
HEADS = 6
HD = 64
TOP = 2
SEQ = 1024
norm_epsilon = 1e-06
masked_score = -1e30
moment_rate = 0.5
average_rate = 0.9
adam_epsilon = 1e-08
weight_decay = 0.1
rate_dense = 0.05
rate_expert = 0.04
rate_small = 0.2


def product(left, right):
    return jnp.dot(left, right, preferred_element_type=jnp.float32)


def left_product(left, right):
    return lax.dot_general(
        left, right, (((0,), (0,)), ((), ())), preferred_element_type=jnp.float32
    )


def right_product(left, right):
    return lax.dot_general(
        left, right, (((1,), (1,)), ((), ())), preferred_element_type=jnp.float32
    )


def normalize(values, gain):
    factor = lax.rsqrt(jnp.mean(values * values, axis=-1, keepdims=True) + norm_epsilon)
    return (values * factor * gain, factor)


def normalize_back(values, factor, gain, grad_out):
    weighted = grad_out * gain
    grad_gain = jnp.sum(grad_out * values * factor, axis=0)
    grad_values = factor * weighted - values * (factor * factor * factor) * jnp.mean(
        weighted * values, axis=-1, keepdims=True
    )
    return (grad_values, grad_gain)


def rotation(position_row):
    frequency = jnp.exp(jnp.arange(HD // 2, dtype=jnp.float32) * (-2.0 * math.log(10000.0) / HD))
    angles = position_row.astype(jnp.float32)[:, None] * frequency[None, :]
    return (jnp.cos(angles)[:, None, :], jnp.sin(angles)[:, None, :])


def rotate(values, cosine, sine_part, direction):
    half_dim = HD // 2
    front_half = values[..., :half_dim]
    back_half = values[..., half_dim:]
    return jnp.concatenate(
        [
            front_half * cosine - direction * back_half * sine_part,
            direction * front_half * sine_part + back_half * cosine,
        ],
        axis=-1,
    )


def make_masks(segment_row, variate_row):
    same_var = (variate_row[:, None] == variate_row[None, :])[None]
    allowed = (segment_row[:, None] == segment_row[None, :])[None]
    return (same_var, allowed)


def raw_scores(queries, key_rows, same_var, allowed, score_bias):
    scores = jnp.einsum(
        "qhd,khd->hqk", queries, key_rows, preferred_element_type=jnp.float32
    ) * HD ** (-0.5)
    scores = scores + jnp.where(
        same_var, score_bias[0][:, None, None], score_bias[1][:, None, None]
    )
    return jnp.where(allowed, scores, masked_score)


def attend_forward(score_bias, packed):
    queries, key_rows, values, segment_row, variate_row = packed
    same_var, allowed = make_masks(segment_row, variate_row)
    scores = raw_scores(queries, key_rows, same_var, allowed, score_bias)
    row_max = jnp.max(scores, axis=-1, keepdims=True)
    weights = jnp.exp(scores - row_max)
    row_total = jnp.sum(weights, axis=-1, keepdims=True)
    probs_low = (weights / row_total).astype(jnp.bfloat16)
    mixed_out = jnp.einsum("hqk,khd->qhd", probs_low, values, preferred_element_type=jnp.float32)
    return (mixed_out.astype(jnp.bfloat16), row_max + jnp.log(row_total))


def attend_backward(score_bias, packed):
    queries, key_rows, values, segment_row, variate_row, summary, grad_mixed = packed
    same_var, allowed = make_masks(segment_row, variate_row)
    probs_full = jnp.exp(raw_scores(queries, key_rows, same_var, allowed, score_bias) - summary)
    grad_probs = jnp.einsum("qhd,khd->hqk", grad_mixed, values, preferred_element_type=jnp.float32)
    grad_values = jnp.einsum(
        "hqk,qhd->khd",
        probs_full.astype(jnp.bfloat16),
        grad_mixed,
        preferred_element_type=jnp.float32,
    )
    row_inner = jnp.sum(probs_full * grad_probs, axis=-1, keepdims=True)
    grad_scores = (probs_full * (grad_probs - row_inner)).astype(jnp.bfloat16)
    score_grads = grad_scores.astype(jnp.float32)
    grad_bias = jnp.stack(
        [
            jnp.sum(jnp.where(same_var, score_grads, 0.0), axis=(1, 2)),
            jnp.sum(jnp.where(same_var, 0.0, score_grads), axis=(1, 2)),
        ]
    )
    grad_queries = jnp.einsum(
        "hqk,khd->qhd", grad_scores, key_rows, preferred_element_type=jnp.float32
    ) * HD ** (-0.5)
    grad_keys = jnp.einsum(
        "hqk,qhd->khd", grad_scores, queries, preferred_element_type=jnp.float32
    ) * HD ** (-0.5)
    return (grad_queries, grad_keys, grad_values, grad_bias)


def to_experts(outgoing):
    return lax.all_to_all(outgoing, "exp", split_axis=0, concat_axis=0, tiled=True)


def from_experts(results):
    return lax.all_to_all(results, "exp", split_axis=0, concat_axis=0, tiled=True)


def expert_forward(arrived, gate_up_low, down_low):
    gate_pre = product(arrived, gate_up_low[0, 0])
    up_pre = product(arrived, gate_up_low[0, 1])
    hidden = (jax.nn.silu(gate_pre) * up_pre).astype(jnp.bfloat16)
    results = product(hidden, down_low[0]).astype(jnp.bfloat16)
    return ((arrived, gate_pre, up_pre, hidden), results)


def expert_backward(stored, grad_arrived, gate_up_low, down_low):
    in_rows, gate_pre, up_pre, hidden = stored
    grad_hidden = right_product(grad_arrived, down_low[0])
    sigmoid = jax.nn.sigmoid(gate_pre)
    grad_gate = (grad_hidden * up_pre * sigmoid * (1.0 + gate_pre * (1.0 - sigmoid))).astype(
        jnp.bfloat16
    )
    grad_up = (grad_hidden * gate_pre * sigmoid).astype(jnp.bfloat16)
    grad_gate_up = jnp.stack([left_product(in_rows, grad_gate), left_product(in_rows, grad_up)])[
        None
    ]
    grad_down = left_product(hidden, grad_arrived)[None]
    grad_in_rows = (
        right_product(grad_gate, gate_up_low[0, 0]) + right_product(grad_up, gate_up_low[0, 1])
    ).astype(jnp.bfloat16)
    grad_gate_up, grad_down = (
        lax.psum_scatter(grad_gate_up, "tp", scatter_dimension=3, tiled=True),
        lax.psum_scatter(grad_down, "tp", scatter_dimension=1, tiled=True),
    )
    return (grad_in_rows, grad_gate_up, grad_down)


def adamw_update(old_state, grad_value, rate, decay, step_value):
    moment_one = moment_rate * old_state[1] + (1.0 - moment_rate) * grad_value
    moment_two = moment_rate * old_state[2] + (1.0 - moment_rate) * grad_value * grad_value
    correction = 1.0 - jnp.power(moment_rate, step_value)
    master = old_state[0] - rate * (
        moment_one / correction / (jnp.sqrt(moment_two / correction) + adam_epsilon)
        + decay * old_state[0]
    )
    average = average_rate * old_state[3] + (1.0 - average_rate) * master
    return jnp.stack([master, moment_one, moment_two, average])


def local(
    tokens,
    cotangent,
    routes,
    segments,
    variates,
    positions,
    step_count,
    dense_state,
    gate_up_state,
    down_state,
    small_state,
):
    tok_count = tokens.shape[0]
    seq_count = segments.shape[0]
    experts = lax.axis_size("exp") * gate_up_state.shape[1]
    capacity = 2 * tok_count * TOP // experts
    flat_weights = lax.all_gather(
        dense_state[0].astype(jnp.bfloat16), ("exp", "tp"), axis=0, tiled=True
    )
    in_proj = flat_weights[: 3 * D * D].reshape(D, 3 * D)
    out_proj = flat_weights[3 * D * D : 4 * D * D].reshape(D, D)
    router_weight = flat_weights[4 * D * D :].reshape(D, experts)
    small_params = small_state[0]
    gain_one = small_params[:D]
    gain_two = small_params[D : 2 * D]
    score_bias = small_params[2 * D :].reshape(2, HEADS)
    gate_up_low = gate_up_state[0].astype(jnp.bfloat16)
    down_low = down_state[0].astype(jnp.bfloat16)
    gate_up_low, down_low = (
        lax.all_gather(gate_up_low, "tp", axis=3, tiled=True),
        lax.all_gather(down_low, "tp", axis=1, tiled=True),
    )
    inputs = tokens.astype(jnp.float32)
    normed_one, scale_one = normalize(inputs, gain_one)
    normed_one = normed_one.astype(jnp.bfloat16)
    projected = product(normed_one, in_proj)
    cosine, sine_part = rotation(positions.reshape(-1))
    queries = rotate(projected[:, :D].reshape(tok_count, HEADS, HD), cosine, sine_part, 1.0).astype(
        jnp.bfloat16
    )
    key_rows = rotate(
        projected[:, D : 2 * D].reshape(tok_count, HEADS, HD), cosine, sine_part, 1.0
    ).astype(jnp.bfloat16)
    values = projected[:, 2 * D :].reshape(tok_count, HEADS, HD).astype(jnp.bfloat16)
    seq_queries = queries.reshape(seq_count, SEQ, HEADS, HD)
    seq_keys = key_rows.reshape(seq_count, SEQ, HEADS, HD)
    seq_values = values.reshape(seq_count, SEQ, HEADS, HD)
    mixed_out, summary = lax.map(
        partial(attend_forward, score_bias), (seq_queries, seq_keys, seq_values, segments, variates)
    )
    mixed_out = mixed_out.reshape(tok_count, D)
    middle = inputs + product(mixed_out, out_proj)
    normed_two, scale_two = normalize(middle, gain_two)
    normed_two = normed_two.astype(jnp.bfloat16)
    logits = product(normed_two, router_weight)
    select = routes[:, :, None] == jnp.arange(experts, dtype=jnp.int32)[None, None, :]
    chosen = jnp.sum(jnp.where(select, logits[:, None, :], 0.0), axis=-1)
    gate_probs = jax.nn.softmax(chosen, axis=-1)
    pair_routes = routes.reshape(-1)
    matches = (pair_routes[:, None] == jnp.arange(experts, dtype=jnp.int32)[None, :]).astype(
        jnp.int32
    )
    slot_rank = jnp.sum((jnp.cumsum(matches, axis=0) - matches) * matches, axis=1)
    slot_index = pair_routes * capacity + slot_rank
    source = (
        jnp.zeros((experts * capacity,), jnp.int32)
        .at[slot_index]
        .set(jnp.arange(tok_count * TOP, dtype=jnp.int32))
    )
    filled = jnp.zeros((experts * capacity,), jnp.int32).at[slot_index].set(1) > 0
    outgoing = jnp.where(filled[:, None], normed_two[source // TOP], 0)
    cot_values = cotangent.astype(jnp.float32)
    grad_pairs = (
        (gate_probs[:, :, None] * cot_values[:, None, :])
        .reshape(tok_count * TOP, D)
        .astype(jnp.bfloat16)
    )
    grad_outgoing = jnp.where(filled[:, None], grad_pairs[source], 0)
    arrived = to_experts(outgoing)
    stored, results = expert_forward(arrived, gate_up_low, down_low)
    returned = from_experts(results)
    grad_arrived = to_experts(grad_outgoing)
    grad_rows, grad_gate_up, grad_down = expert_backward(
        stored, grad_arrived, gate_up_low, down_low
    )
    grad_returned = from_experts(grad_rows)
    out_pairs = returned[slot_index].astype(jnp.float32).reshape(tok_count, TOP, D)
    block_out = (middle + jnp.sum(gate_probs[:, :, None] * out_pairs, axis=1)).astype(jnp.bfloat16)
    grad_gate = jnp.sum(cot_values[:, None, :] * out_pairs, axis=-1)
    grad_chosen = gate_probs * (grad_gate - jnp.sum(gate_probs * grad_gate, axis=-1, keepdims=True))
    grad_logits = jnp.sum(jnp.where(select, grad_chosen[:, :, None], 0.0), axis=1).astype(
        jnp.bfloat16
    )
    back_pairs = grad_returned[slot_index].astype(jnp.float32).reshape(tok_count, TOP, D)
    grad_normed_two = right_product(grad_logits, router_weight) + jnp.sum(back_pairs, axis=1)
    grad_router = left_product(normed_two, grad_logits)
    grad_middle, grad_gain_two = normalize_back(middle, scale_two, gain_two, grad_normed_two)
    grad_middle = grad_middle + cot_values
    grad_branch = grad_middle.astype(jnp.bfloat16)
    grad_out_proj = left_product(mixed_out, grad_branch)
    grad_mixed = (
        right_product(grad_branch, out_proj).astype(jnp.bfloat16).reshape(seq_count, SEQ, HEADS, HD)
    )
    grad_queries, grad_keys, grad_values, grad_bias = lax.map(
        partial(attend_backward, score_bias),
        (seq_queries, seq_keys, seq_values, segments, variates, summary, grad_mixed),
    )
    grad_bias = jnp.sum(grad_bias, axis=0)
    grad_queries = rotate(
        grad_queries.reshape(tok_count, HEADS, HD), cosine, sine_part, -1.0
    ).reshape(tok_count, D)
    grad_keys = rotate(grad_keys.reshape(tok_count, HEADS, HD), cosine, sine_part, -1.0).reshape(
        tok_count, D
    )
    grad_projected = jnp.concatenate(
        [grad_queries, grad_keys, grad_values.reshape(tok_count, D)], axis=1
    ).astype(jnp.bfloat16)
    grad_in_proj = left_product(normed_one, grad_projected)
    grad_normed_one = right_product(grad_projected, in_proj)
    grad_inputs, grad_gain_one = normalize_back(inputs, scale_one, gain_one, grad_normed_one)
    grad_in = (grad_middle + grad_inputs).astype(jnp.bfloat16)
    dense_grad = jnp.concatenate(
        [grad_in_proj.reshape(-1), grad_out_proj.reshape(-1), grad_router.reshape(-1)]
    )
    dense_grad = lax.psum_scatter(dense_grad, ("exp", "tp"), scatter_dimension=0, tiled=True)
    small_grad = lax.psum(
        jnp.concatenate([grad_gain_one, grad_gain_two, grad_bias.reshape(-1)]), ("exp", "tp")
    )
    step_value = step_count[0].astype(jnp.float32)
    dense_new = adamw_update(dense_state, dense_grad, rate_dense, weight_decay, step_value)
    gate_up_new = adamw_update(gate_up_state, grad_gate_up, rate_expert, weight_decay, step_value)
    down_new = adamw_update(down_state, grad_down, rate_expert, weight_decay, step_value)
    small_new = adamw_update(small_state, small_grad, rate_small, 0.0, step_value)
    return (
        block_out,
        grad_in,
        dense_new,
        dense_new[0].astype(jnp.bfloat16),
        gate_up_new,
        gate_up_new[0].astype(jnp.bfloat16),
        down_new,
        down_new[0].astype(jnp.bfloat16),
        small_new,
    )


def solution(mesh):
    in_specs = (
        P(("exp", "tp"), None),
        P(("exp", "tp"), None),
        P(("exp", "tp"), None),
        P(("exp", "tp"), None),
        P(("exp", "tp"), None),
        P(("exp", "tp"), None),
        P(),
        P(None, ("exp", "tp")),
        P(None, "exp", None, None, "tp"),
        P(None, "exp", "tp", None),
        P(),
    )
    out_specs = (
        P(("exp", "tp"), None),
        P(("exp", "tp"), None),
        P(None, ("exp", "tp")),
        P(("exp", "tp")),
        P(None, "exp", None, None, "tp"),
        P("exp", None, None, "tp"),
        P(None, "exp", "tp", None),
        P("exp", "tp", None),
        P(),
    )
    return jax.shard_map(local, mesh=mesh, in_specs=in_specs, out_specs=out_specs, check_vma=False)
```

profile of v0, /device:TPU:0, one launch (start us, length us, event | category | flops | bytes accessed | tf_op | source)
XLA Modules:
  0.0 1325.2 jit_solution(2155927653004741738)
XLA Ops:
  76.0 70.9 %all-reduce.5.cloned.1.call-done = bf16[592896]{0:T(1024)(128)(2,1)} async-done(((bf16[592896]{0:T(1024)(128)(2,1)}), bf16[592896]{0:T(1024)(128)(2,1)}) %all-reduce.5.cloned.1.call-update) | async-done | bytes 1185808
  182.2 85.0 %while.28 = (s32[]{:T(128)}, bf16[2,1024,6,64]{1,3,2,0:T(8,128)(2,1)}, f32[2,6,1024,1]{2,1,3,0:T(8,128)S(1)}, bf16[2,1024,6,64]{1,3,2,0:T(8,128)(2,1)}, s32[2,10...) while((s32[]{:T(128)}, ...), condition=%wide.region_4.5_spmd, body=%wide.region_1.4_spmd.sunk | while | flops 1726343168 | bytes 106172760 | solution.py:228
  284.8 34.8 %gather_fusion.2 = bf16[8192,384]{1,0:T(8,128)(2,1)} fusion(bf16[4096,384]{1,0:T(8,128)(2,1)} %multiply_convert_fusion.4, s32[8192]{0:T(1024)S(1)} %copy-done.59), kind=kCustom, calls=%fused_computation.2 | custom fusion | bytes 12615680 | tf_op jit(solution)/shard_map/gather | solution.py:258
  319.5 33.1 %gather_fusion = bf16[8192,384]{1,0:T(8,128)(2,1)} fusion(bf16[2048,384]{1,0:T(8,128)(2,1)S(1)} %copy.148, s32[8192]{0:T(1024)S(1)} %copy-done.58), kind=kCustom, calls=%fused_computation | custom fusion | bytes 12615680 | tf_op jit(solution)/shard_map/gather | solution.py:251
  361.6 74.9 %all_to_all.42 = bf16[8,1024,384]{2,1,0:T(8,128)(2,1)} all-to-all(bf16[8,1024,384]{2,1,0:T(8,128)(2,1)S(1)} %get-tuple-element.412), channel_id=1, replica_groups=mesh['exp'=8,'tp'=4] {'exp'}, dimensions={0} | all-to-all | bytes 12582912 | tf_op jit(solution)/shard_map/all_to_all | solution.py:131
  458.4 18.0 %all_gather.10 = bf16[1,2,384,512]{3,2,1,0:T(8,128)(2,1)S(1)} all-gather(bf16[1,2,384,128]{3,2,1,0:T(8,128)(2,1)S(1)} %bitcast_convert_fusion), channel_id=1, replica_groups=mesh['exp'=8,'tp'=4] {'tp'}, dimensions={3}, use_global_device_ids=true | all-gather | bytes 983040 | tf_op jit(solution)/shard_map/all_gather | solution.py:210
  512.9 26.0 %multiply_convert_fusion.1 = (bf16[8192,512]{1,0:T(8,128)(2,1)}, bf16[8192,512]{1,0:T(8,128)(2,1)}, bf16[8192,512]{1,0:T(8,128)(2,1)}) fusion(f32[8192,512]{1,0:T(8,128)} %fusion.69, f32[8192,512]{1,0:T(8,128)} %fusion.70, bf16[8192,384]{1,0:T(8,128)(2,1)} %bitcast.43, bf16[1,512,384]{2,1,0:T(8,128)(2,1)S(1)} %all_gather.11), kind=kOutput, calls=%fused_computation.74 | convolution fusion | flops 3288334336 | bytes 65404928 | tf_op jit(solution)/shard_map/dot_general | solution.py:35
  582.9 50.4 %all-to-all-done.3 = bf16[8,1024,384]{2,1,0:T(8,128)(2,1)} async-done(((bf16[8,1024,384]{2,1,0:T(8,128)(2,1)}), bf16[8,1024,384]{2,1,0:T(8,128)(2,1)}, u32[]{:S(2)}, u32[]{:S(2)}) %all-to-all-start.3) | async-done | bytes 6291488 | tf_op jit(solution)/shard_map/all_to_all | solution.py:135
  659.6 32.7 %reduce-scatter.3.cloned.1.call-done = f32[1,2,384,128]{3,2,1,0:T(8,128)} async-done(((f32[1,2,384,512]{3,2,1,0:T(8,128)}), f32[1,2,384,128]{3,2,1,0:T(8,128)}) %reduce-scatter.3.cloned.1.call-update) | async-done | bytes 393232 | tf_op jit(solution)/shard_map/reduce_scatter | solution.py:162
  695.5 17.6 %gather_fusion.3 = bf16[4096,384]{1,0:T(8,128)(2,1)S(1)} fusion(bf16[8192,384]{1,0:T(8,128)(2,1)} %bitcast.45, s32[4096]{0:T(1024)S(1)} %broadcast_clamp_fusion), kind=kCustom, calls=%fused_computation.3 | custom fusion | bytes 6307840 | tf_op jit(solution)/shard_map/gather | solution.py:274
  717.9 27.3 %reduce_sum.183 = f32[2048,384]{1,0:T(8,128)S(1)} reduce(f32[2048,2,384]{2,1,0:T(2,128)} %reshape.700, f32[]{:T(128)} %constant.55.clone.1), dimensions={1}, to_apply=%region_18.19 | reduce | flops 786432 | bytes 9437188 | tf_op jit(solution)/shard_map/reduce_sum | solution.py:275
  747.7 17.6 %gather_fusion.1 = bf16[4096,384]{1,0:T(8,128)(2,1)S(1)} fusion(bf16[8192,384]{1,0:T(8,128)(2,1)} %bitcast.41, s32[4096]{0:T(1024)S(1)} %broadcast_clamp_fusion), kind=kCustom, calls=%fused_computation.1 | custom fusion | bytes 6307840 | tf_op jit(solution)/shard_map/gather | solution.py:267
  770.0 19.8 %multiply_reduce_fusion.1 = (f32[2048,2]{1,0:T(8,128)}, f32[2048,384]{1,0:T(8,128)}) fusion(f32[2048,2,384]{2,1,0:T(2,128)} %reshape.699, f32[2048,384]{1,0:T(8,128)} %copy.151, f32[2048,2]{1,0:T(8,128)} %copy.144), kind=kLoop, calls=%fused_computation.87 | loop fusion | flops 5500928 | bytes 12615680 | tf_op jit(solution)/shard_map/reduce_sum | solution.py:269
  815.5 290.6 %while.29 = (s32[]{:T(128)}, f32[2,1024,6,64]{1,0,3,2:T(2,128)}, f32[2,1024,6,64]{1,0,3,2:T(2,128)}, bf16[2,1024,6,64]{1,3,2,0:T(8,128)(2,1)}, f32[2,2,6]{2,1,0:...) while((s32[]{:T(128)}, f32[2,1024,6,64]{1,0,3,2:T(2,128)}, ...), condition=%wide.region_24.25_spmd, body=%wide.region_20.24_spmd.sunk | while | flops 4130072576 | bytes 286152160 | solution.py:284
  830.2 20.6 %multiply_reduce_fusion.14 = (f32[6,1024]{1,0:T(8,128)S(1)}, f32[6,1024,1024]{1,2,0:T(8,128)}) fusion(f32[6,1024,1024]{1,2,0:T(8,128)} %fusion.160, f32[6,1024]{1,0:T(8,128)S(1)} %dynamic-slice_bitcast_fusion.2, f32[6]{0:T(128)S(1)} %get-tuple-element.575, f32[6]{0:T(128)S(1)} %get-tuple-element.576, ...), kind=kOutput, calls=%fused_computation.38.clone.1 | convolution fusion | flops 849340416 | bytes 54051888 | tf_op jit(solution)/shard_map/while/body/eval_jaxpr/qhd,khd->hqk/dot_general | solution.py:80
  850.8 23.3 %fusion.161 = (f32[6]{0:T(128)S(1)}, f32[6]{0:T(128)S(1)}, bf16[6,1024,1024]{1,2,0:T(8,128)(2,1)}) fusion(pred[1024,1024]{0,1:T(8,128)(4,1)S(1)} %broadcast_compare_fusion.11, f32[6,1024,1024]{1,2,0:T(8,128)} %get-tuple-element.578, f32[6,1024,1024]{1,2,0:T(8,128)} %fusion.160, f32[6,1024]{1,0:T(8,128)S(1)} %get-tuple-element.579), kind=kLoop, calls=%fused_computation.35.clone.1 | loop fusion | flops 50331632 | bytes 63987760 | tf_op jit(solution)/shard_map/while/body/eval_jaxpr/reduce_sum | solution.py:117
  905.5 27.8 %dynamic_update_slice.37 = f32[2,1024,6,64]{1,0,3,2:T(2,128)} dynamic-update-slice(f32[2,1024,6,64]{1,0,3,2:T(2,128)} %get-tuple-element.630, f32[1,1024,6,64]{1,0,3,2:T(1,128)} %copy.205, s32[]{:T(128)S(6)} %copy.228, s32[]{:T(128)} %constant.51.clone.1..sunk, s32[]{:T(128)} %constant.51.clone.1..sunk, s32[]{:T(128)} %constant.51.clone.1..sunk) | dynamic-update-slice | bytes 3145732 | tf_op jit(solution)/shard_map/while/body/jit(dynamic_update_index_in_dim)/dynamic_update_slice | solution.py:284
  933.3 27.5 %dynamic_update_slice.36 = f32[2,1024,6,64]{1,0,3,2:T(2,128)} dynamic-update-slice(f32[2,1024,6,64]{1,0,3,2:T(2,128)} %get-tuple-element.629, f32[1,1024,6,64]{1,0,3,2:T(1,128)S(1)} %copy-done.1, s32[]{:T(128)S(6)} %copy.228, s32[]{:T(128)} %constant.51.clone.1..sunk, s32[]{:T(128)} %constant.51.clone.1..sunk, s32[]{:T(128)} %constant.51.clone.1..sunk) | dynamic-update-slice | bytes 3145732 | tf_op jit(solution)/shard_map/while/body/jit(dynamic_update_index_in_dim)/dynamic_update_slice | solution.py:284
  975.3 20.6 %multiply_reduce_fusion.14 = (f32[6,1024]{1,0:T(8,128)S(1)}, f32[6,1024,1024]{1,2,0:T(8,128)}) fusion(f32[6,1024,1024]{1,2,0:T(8,128)} %fusion.160, f32[6,1024]{1,0:T(8,128)S(1)} %dynamic-slice_bitcast_fusion.2, f32[6]{0:T(128)S(1)} %get-tuple-element.575, f32[6]{0:T(128)S(1)} %get-tuple-element.576, ...), kind=kOutput, calls=%fused_computation.38.clone.1 | convolution fusion | flops 849340416 | bytes 54051888 | tf_op jit(solution)/shard_map/while/body/eval_jaxpr/qhd,khd->hqk/dot_general | solution.py:80
  995.9 23.3 %fusion.161 = (f32[6]{0:T(128)S(1)}, f32[6]{0:T(128)S(1)}, bf16[6,1024,1024]{1,2,0:T(8,128)(2,1)}) fusion(pred[1024,1024]{0,1:T(8,128)(4,1)S(1)} %broadcast_compare_fusion.11, f32[6,1024,1024]{1,2,0:T(8,128)} %get-tuple-element.578, f32[6,1024,1024]{1,2,0:T(8,128)} %fusion.160, f32[6,1024]{1,0:T(8,128)S(1)} %get-tuple-element.579), kind=kLoop, calls=%fused_computation.35.clone.1 | loop fusion | flops 50331632 | bytes 63987760 | tf_op jit(solution)/shard_map/while/body/eval_jaxpr/reduce_sum | solution.py:117
  1050.6 27.8 %dynamic_update_slice.37 = f32[2,1024,6,64]{1,0,3,2:T(2,128)} dynamic-update-slice(f32[2,1024,6,64]{1,0,3,2:T(2,128)} %get-tuple-element.630, f32[1,1024,6,64]{1,0,3,2:T(1,128)} %copy.205, s32[]{:T(128)S(6)} %copy.228, s32[]{:T(128)} %constant.51.clone.1..sunk, s32[]{:T(128)} %constant.51.clone.1..sunk, s32[]{:T(128)} %constant.51.clone.1..sunk) | dynamic-update-slice | bytes 3145732 | tf_op jit(solution)/shard_map/while/body/jit(dynamic_update_index_in_dim)/dynamic_update_slice | solution.py:284
  1078.4 27.5 %dynamic_update_slice.36 = f32[2,1024,6,64]{1,0,3,2:T(2,128)} dynamic-update-slice(f32[2,1024,6,64]{1,0,3,2:T(2,128)} %get-tuple-element.629, f32[1,1024,6,64]{1,0,3,2:T(1,128)S(1)} %copy-done.1, s32[]{:T(128)S(6)} %copy.228, s32[]{:T(128)} %constant.51.clone.1..sunk, s32[]{:T(128)} %constant.51.clone.1..sunk, s32[]{:T(128)} %constant.51.clone.1..sunk) | dynamic-update-slice | bytes 3145732 | tf_op jit(solution)/shard_map/while/body/jit(dynamic_update_index_in_dim)/dynamic_update_slice | solution.py:284
  1136.9 39.5 %psum.7 = f32[780]{0:T(1024)S(1)} all-reduce(f32[780]{0:T(1024)S(1)} %pad_maximum_fusion.12), channel_id=1, replica_groups=mesh['exp'=8,'tp'=4] {'exp','tp'}, use_global_device_ids=true, to_apply=%region_32.33 | all-reduce | flops 780 | bytes 6240 | tf_op jit(solution)/shard_map/psum | solution.py:306
  1186.8 128.5 %all-reduce.7.cloned.1.call-done = f32[592896]{0:T(1024)} async-done(((f32[592896]{0:T(1024)}), f32[592896]{0:T(1024)}) %all-reduce.7.cloned.1.call-update) | async-done | bytes 2371600
  (386 shorter events, 518.2 us)
Async XLA Ops:
  7.2 139.7 %all-reduce.5.cloned.1.call-start = ((), (), s32[]{:S(2)}) async-start(), calls=%async_computation.8 | async-start | bytes 2371584
  12.9 38.2 %copy-start.28 = (bf16[2048,384]{1,0:T(8,128)(2,1)S(1)}, bf16[2048,384]{1,0:T(8,128)(2,1)}, u32[]{:S(2)}) copy-start(bf16[2048,384]{1,0:T(8,128)(2,1)} %param.15) | copy-start | bytes 4718596
  19.0 31.4 %copy-start.66 = (s32[4096,1]{0,1:T(1,128)}, s32[4096,1]{0,1:T(1,128)S(1)}, u32[]{:S(2)}) copy-start(s32[4096,1]{0,1:T(1,128)S(1)} %compare_select_fusion) | copy-start | bytes 49156
  51.8 97.3 %copy-start.4 = (bf16[2048,384]{0,1:T(8,128)(2,1)}, bf16[2048,384]{0,1:T(8,128)(2,1)S(1)}, u32[]{:S(2)}) copy-start(bf16[2048,384]{0,1:T(8,128)(2,1)S(1)} %copy.139) | copy-start | bytes 4718596
  53.0 96.2 %copy-start.56 = (f32[2048]{0:T(1024)}, f32[2048]{0:T(1024)S(1)}, u32[]{:S(2)}) copy-start(f32[2048]{0:T(1024)S(1)} %get-tuple-element.408) | copy-start | bytes 24580
  74.1 77.8 %copy-start.68 = (f32[384]{0:T(512)}, f32[384]{0:T(512)S(1)}, u32[]{:S(2)}) copy-start(f32[384]{0:T(512)S(1)} %get-tuple-element.305) | copy-start | bytes 4612
  284.8 34.8 %copy-start.58 = (s32[8192]{0:T(1024)S(1)}, s32[8192]{0:T(1024)}, u32[]{:S(2)}) copy-start(s32[8192]{0:T(1024)} %get-tuple-element.403) | copy-start | bytes 98308
  319.5 33.1 %copy-start.74 = (pred[8,1024]{1,0:T(8,128)(4,1)S(1)}, pred[8,1024]{1,0:T(8,128)(4,1)}, u32[]{:S(2)}) copy-start(pred[8,1024]{1,0:T(8,128)(4,1)} %broadcast_in_dim.212) | copy-start | bytes 24580
  436.5 76.4 %all-to-all-start.2 = ((bf16[8,1024,384]{2,1,0:T(8,128)(2,1)}), bf16[8,1024,384]{2,1,0:T(8,128)(2,1)}, u32[]{:S(2)}, u32[]{:S(2)}) async-start(bf16[8,1024,384]{2,1,0:T(8,128)(2,1)} %get-tuple-element.411), calls=%async_computation.2 | async-start | bytes 12582912 | tf_op jit(solution)/shard_map/all_to_all | solution.py:131
  458.3 29.7 %slice-start = ((s8[6291456]{0:T(1024)(128)(4,1)}), s8[4194304]{0:T(1024)(128)(4,1)S(1)}, s32[]{:S(2)}) async-start(s8[6291456]{0:T(1024)(128)(4,1)} %bitcast.320), calls=%async_computation.10 | async-start | bytes 8388608
  556.9 76.4 %all-to-all-start.3 = ((bf16[8,1024,384]{2,1,0:T(8,128)(2,1)}), bf16[8,1024,384]{2,1,0:T(8,128)(2,1)}, u32[]{:S(2)}, u32[]{:S(2)}) async-start(bf16[8,1024,384]{2,1,0:T(8,128)(2,1)} %bitcast.323), calls=%async_computation.3 | async-start | bytes 12582912 | tf_op jit(solution)/shard_map/all_to_all | solution.py:135
  561.7 95.2 %reduce-scatter.5.cloned.1.call-start = ((), (), s32[]{:S(2)}) async-start(), calls=%async_computation.7 | async-start | bytes 983040 | tf_op jit(solution)/shard_map/reduce_scatter | solution.py:163
  633.3 114.4 %all-to-all-start.1 = ((bf16[8,1024,384]{2,1,0:T(8,128)(2,1)}), bf16[8,1024,384]{2,1,0:T(8,128)(2,1)}, u32[]{:S(2)}, u32[]{:S(2)}) async-start(bf16[8,1024,384]{2,1,0:T(8,128)(2,1)} %bitcast.330), calls=%async_computation.1 | async-start | bytes 12582912 | tf_op jit(solution)/shard_map/all_to_all | solution.py:135
  638.3 53.9 %reduce-scatter.3.cloned.1.call-start = ((), (), s32[]{:S(2)}) async-start(), calls=%async_computation.6 | async-start | bytes 1966080 | tf_op jit(solution)/shard_map/reduce_scatter | solution.py:162
  655.3 37.0 %copy-start.27 = (f32[4,1,2,384,128]{4,3,2,1,0:T(8,128)S(1)}, f32[4,1,2,384,128]{4,3,2,1,0:T(8,128)}, u32[]{:S(2)}) copy-start(f32[4,1,2,384,128]{4,3,2,1,0:T(8,128)} %param.23) | copy-start | bytes 4718596
  655.3 660.0 %all-reduce.7.cloned.1.call-start = ((), (), s32[]{:S(2)}) async-start(), calls=%async_computation.9 | async-start | bytes 4743168
  770.0 24.2 %copy-start.3 = (f32[2048,384]{0,1:T(8,128)S(1)}, f32[2048,384]{0,1:T(8,128)}, u32[]{:S(2)}) copy-start(f32[2048,384]{0,1:T(8,128)} %copy-done.2) | copy-start | bytes 9437188
  770.0 24.1 %copy-start.63 = (f32[2048]{0:T(1024)S(1)}, f32[2048]{0:T(1024)}, u32[]{:S(2)}) copy-start(f32[2048]{0:T(1024)} %copy-done.62) | copy-start | bytes 24580
  905.5 27.8 %copy-start.1 = (f32[1,1024,6,64]{1,0,3,2:T(1,128)S(1)}, f32[1,1024,6,64]{1,0,3,2:T(1,128)}, u32[]{:S(2)}) copy-start(f32[1,1024,6,64]{1,0,3,2:T(1,128)} %copy.204) | copy-start | bytes 4718596 | tf_op jit(solution)/shard_map/while
  1050.6 27.8 %copy-start.1 = (f32[1,1024,6,64]{1,0,3,2:T(1,128)S(1)}, f32[1,1024,6,64]{1,0,3,2:T(1,128)}, u32[]{:S(2)}) copy-start(f32[1,1024,6,64]{1,0,3,2:T(1,128)} %copy.204) | copy-start | bytes 4718596 | tf_op jit(solution)/shard_map/while
  1184.6 130.7 %copy-start.38 = (f32[18528]{0:T(1024)S(1)}, f32[18528]{0:T(1024)}, u32[]{:S(2)}) copy-start(f32[18528]{0:T(1024)} %copy-done.37) | copy-start | bytes 222340
  1184.6 130.7 %copy-start.44 = (f32[18528]{0:T(1024)S(1)}, f32[18528]{0:T(1024)}, u32[]{:S(2)}) copy-start(f32[18528]{0:T(1024)} %get-tuple-element.296) | copy-start | bytes 222340
  1184.6 130.7 %copy-start.45 = (f32[18528]{0:T(1024)S(1)}, f32[18528]{0:T(1024)}, u32[]{:S(2)}) copy-start(f32[18528]{0:T(1024)} %get-tuple-element.297) | copy-start | bytes 222340
  1184.6 132.4 %copy-start.43 = (f32[18528]{0:T(1024)S(1)}, f32[18528]{0:T(1024)}, u32[]{:S(2)}) copy-start(f32[18528]{0:T(1024)} %get-tuple-element.299) | copy-start | bytes 222340
  (75 other events, 448.3 us)
Sparse Core Ops, SparseCore 0:
  14.0 132.7 all-reduce.4
  572.4 24.7 reduce-scatter.4
  655.4 36.7 reduce-scatter.2
  1180.7 134.5 all-reduce.6
where the time goes:
time: 1340 us; the launch traced here: 1330 us
  local copies, waits for them, and re-layouts  366 us (27%)
  waiting for transfers between devices  299 us (22%)
  matrix products  294 us (22%)
  other arithmetic  186 us (14%)
  blocking collectives  147 us (11%)
  between operations  16.3 us (1%)
  starting transfers between devices  14.7 us (1%)
    unnamed x6, waiting for transfers between devices  199 us
    dynamic_update_slice x8, local copies, waits for them, and re-layouts, local(): lax.map(partial(attend_backward, score_bias), (seq_queries, seq_keys, seq...  122 us
    all_to_all x1, blocking collectives, to_experts(): lax.all_to_all(outgoing, 'exp', split_axis=0, concat_axis=0, tiled=True)  74.9 us
    dot_general x4, matrix products, raw_scores(): jnp.einsum('qhd,khd->hqk', queries, key_rows, preferred_element_type=jnp....  67.9 us
    dot_general x6, matrix products, right_product(): lax.dot_general(left, right, (((1,), (1,)), ((), ())), preferred_element_...  54.4 us
    all_to_all x2, waiting for transfers between devices, from_experts(): lax.all_to_all(results, 'exp', split_axis=0, concat_axis=0, tiled=True)  50.4 us
    reduce_sum x2, other arithmetic, attend_backward(): jnp.sum(jnp.where(same_var, score_grads, 0.0), axis=(1, 2))  46.5 us
    psum x1, blocking collectives, local(): lax.psum(jnp.concatenate([grad_gain_one, grad_gain_two, grad_bias.reshape...  39.5 us
  transfers between devices with their start and end apart: 7, of which 5 were waited for; matrix products, arithmetic and copies ran while one was open for 14% of the time, Pallas kernels for 0%

commit v1 on v0

--- a/solution.py
+++ b/solution.py
@@ -303,9 +303,10 @@
         [grad_in_proj.reshape(-1), grad_out_proj.reshape(-1), grad_router.reshape(-1)]
     )
     dense_grad = lax.psum_scatter(dense_grad, ("exp", "tp"), scatter_dimension=0, tiled=True)
-    small_grad = lax.psum(
-        jnp.concatenate([grad_gain_one, grad_gain_two, grad_bias.reshape(-1)]), ("exp", "tp")
-    )
+    partial_2 = lax.psum(
+        jnp.concatenate([grad_gain_one, grad_gain_two, grad_bias.reshape(-1)]), "tp"
+    )
+    small_grad = lax.psum(partial_2, "exp")
     step_value = step_count[0].astype(jnp.float32)
     dense_new = adamw_update(dense_state, dense_grad, rate_dense, weight_decay, step_value)
     gate_up_new = adamw_update(gate_up_state, grad_gate_up, rate_expert, weight_decay, step_value)

time: 1340 us -> 1320 us (0.985)
  blocking collectives: 147 us -> 130 us
    psum x1, blocking collectives: 39.5 us -> 9.76 us  [local(): lax.psum(jnp.concatenate([grad_gain_one, grad_gain_two, grad_bias.reshape...]
where the time goes in v1:
time: 1320 us; the launch traced here: 1310 us
  local copies, waits for them, and re-layouts  367 us (28%)
  waiting for transfers between devices  297 us (22%)
  matrix products  294 us (22%)
  other arithmetic  186 us (14%)
  blocking collectives  130 us (10%)
  between operations  16.3 us (1%)
  starting transfers between devices  14.7 us (1%)
    unnamed x6, waiting for transfers between devices  197 us
    dynamic_update_slice x8, local copies, waits for them, and re-layouts, local(): lax.map(partial(attend_backward, score_bias), (seq_queries, seq_keys, seq...  122 us
    all_to_all x1, blocking collectives, to_experts(): lax.all_to_all(outgoing, 'exp', split_axis=0, concat_axis=0, tiled=True)  74.9 us
    dot_general x4, matrix products, raw_scores(): jnp.einsum('qhd,khd->hqk', queries, key_rows, preferred_element_type=jnp....  67.6 us
    dot_general x6, matrix products, right_product(): lax.dot_general(left, right, (((1,), (1,)), ((), ())), preferred_element_...  54.5 us
    all_to_all x2, waiting for transfers between devices, from_experts(): lax.all_to_all(results, 'exp', split_axis=0, concat_axis=0, tiled=True)  50.4 us
    reduce_sum x2, other arithmetic, attend_backward(): jnp.sum(jnp.where(same_var, score_grads, 0.0), axis=(1, 2))  46.5 us
    gather x1, local copies, waits for them, and re-layouts, local(): grad_outgoing = jnp.where(filled[:, None], grad_pairs[source], 0)  34.9 us
  transfers between devices with their start and end apart: 7, of which 5 were waited for; matrix products, arithmetic and copies ran while one was open for 14% of the time, Pallas kernels for 0%

profile of v1, /device:TPU:0, one launch (start us, length us, event | category | flops | bytes accessed | tf_op | source)
XLA Modules:
  0.0 1305.5 jit_solution(1225232878444044)
XLA Ops:
  75.9 71.0 %all-reduce.5.cloned.1.call-done = bf16[592896]{0:T(1024)(128)(2,1)} async-done(((bf16[592896]{0:T(1024)(128)(2,1)}), bf16[592896]{0:T(1024)(128)(2,1)}) %all-reduce.5.cloned.1.call-update) | async-done | bytes 1185808
  182.3 84.8 %while.28 = (s32[]{:T(128)}, bf16[2,1024,6,64]{1,3,2,0:T(8,128)(2,1)}, f32[2,6,1024,1]{2,1,3,0:T(8,128)S(1)}, bf16[2,1024,6,64]{1,3,2,0:T(8,128)(2,1)}, s32[2,10...) while((s32[]{:T(128)}, ...), condition=%wide.region_4.5_spmd, body=%wide.region_1.4_spmd.sunk | while | flops 1726343168 | bytes 106172760 | solution.py:228
  284.7 34.9 %gather_fusion.2 = bf16[8192,384]{1,0:T(8,128)(2,1)} fusion(bf16[4096,384]{1,0:T(8,128)(2,1)} %multiply_convert_fusion.4, s32[8192]{0:T(1024)S(1)} %copy-done.59), kind=kCustom, calls=%fused_computation.2 | custom fusion | bytes 12615680 | tf_op jit(solution)/shard_map/gather | solution.py:258
  319.6 33.3 %gather_fusion = bf16[8192,384]{1,0:T(8,128)(2,1)} fusion(bf16[2048,384]{1,0:T(8,128)(2,1)S(1)} %copy.148, s32[8192]{0:T(1024)S(1)} %copy-done.58), kind=kCustom, calls=%fused_computation | custom fusion | bytes 12615680 | tf_op jit(solution)/shard_map/gather | solution.py:251
  361.9 74.9 %all_to_all.42 = bf16[8,1024,384]{2,1,0:T(8,128)(2,1)} all-to-all(bf16[8,1024,384]{2,1,0:T(8,128)(2,1)S(1)} %get-tuple-element.412), channel_id=1, replica_groups=mesh['exp'=8,'tp'=4] {'exp'}, dimensions={0} | all-to-all | bytes 12582912 | tf_op jit(solution)/shard_map/all_to_all | solution.py:131
  458.6 18.0 %all_gather.10 = bf16[1,2,384,512]{3,2,1,0:T(8,128)(2,1)S(1)} all-gather(bf16[1,2,384,128]{3,2,1,0:T(8,128)(2,1)S(1)} %bitcast_convert_fusion), channel_id=1, replica_groups=mesh['exp'=8,'tp'=4] {'tp'}, dimensions={3}, use_global_device_ids=true | all-gather | bytes 983040 | tf_op jit(solution)/shard_map/all_gather | solution.py:210
  496.4 16.7 %all-to-all-done.2 = bf16[8,1024,384]{2,1,0:T(8,128)(2,1)} async-done(((bf16[8,1024,384]{2,1,0:T(8,128)(2,1)}), bf16[8,1024,384]{2,1,0:T(8,128)(2,1)}, u32[]{:S(2)}, u32[]{:S(2)}) %all-to-all-start.2) | async-done | bytes 6291488 | tf_op jit(solution)/shard_map/all_to_all | solution.py:131
  513.2 26.0 %multiply_convert_fusion.1 = (bf16[8192,512]{1,0:T(8,128)(2,1)}, bf16[8192,512]{1,0:T(8,128)(2,1)}, bf16[8192,512]{1,0:T(8,128)(2,1)}) fusion(f32[8192,512]{1,0:T(8,128)} %fusion.69, f32[8192,512]{1,0:T(8,128)} %fusion.70, bf16[8192,384]{1,0:T(8,128)(2,1)} %bitcast.43, bf16[1,512,384]{2,1,0:T(8,128)(2,1)S(1)} %all_gather.11), kind=kOutput, calls=%fused_computation.74 | convolution fusion | flops 3288334336 | bytes 65404928 | tf_op jit(solution)/shard_map/dot_general | solution.py:35
  583.2 50.4 %all-to-all-done.3 = bf16[8,1024,384]{2,1,0:T(8,128)(2,1)} async-done(((bf16[8,1024,384]{2,1,0:T(8,128)(2,1)}), bf16[8,1024,384]{2,1,0:T(8,128)(2,1)}, u32[]{:S(2)}, u32[]{:S(2)}) %all-to-all-start.3) | async-done | bytes 6291488 | tf_op jit(solution)/shard_map/all_to_all | solution.py:135
  659.9 32.6 %reduce-scatter.3.cloned.1.call-done = f32[1,2,384,128]{3,2,1,0:T(8,128)} async-done(((f32[1,2,384,512]{3,2,1,0:T(8,128)}), f32[1,2,384,128]{3,2,1,0:T(8,128)}) %reduce-scatter.3.cloned.1.call-update) | async-done | bytes 393232 | tf_op jit(solution)/shard_map/reduce_scatter | solution.py:162
  695.8 17.6 %gather_fusion.3 = bf16[4096,384]{1,0:T(8,128)(2,1)S(1)} fusion(bf16[8192,384]{1,0:T(8,128)(2,1)} %bitcast.45, s32[4096]{0:T(1024)S(1)} %broadcast_clamp_fusion), kind=kCustom, calls=%fused_computation.3 | custom fusion | bytes 6307840 | tf_op jit(solution)/shard_map/gather | solution.py:274
  718.2 27.3 %reduce_sum.183 = f32[2048,384]{1,0:T(8,128)S(1)} reduce(f32[2048,2,384]{2,1,0:T(2,128)} %reshape.700, f32[]{:T(128)} %constant.55.clone.1), dimensions={1}, to_apply=%region_18.19 | reduce | flops 786432 | bytes 9437188 | tf_op jit(solution)/shard_map/reduce_sum | solution.py:275
  748.0 17.6 %gather_fusion.1 = bf16[4096,384]{1,0:T(8,128)(2,1)S(1)} fusion(bf16[8192,384]{1,0:T(8,128)(2,1)} %bitcast.41, s32[4096]{0:T(1024)S(1)} %broadcast_clamp_fusion), kind=kCustom, calls=%fused_computation.1 | custom fusion | bytes 6307840 | tf_op jit(solution)/shard_map/gather | solution.py:267
  770.4 19.8 %multiply_reduce_fusion.1 = (f32[2048,2]{1,0:T(8,128)}, f32[2048,384]{1,0:T(8,128)}) fusion(f32[2048,2,384]{2,1,0:T(2,128)} %reshape.699, f32[2048,384]{1,0:T(8,128)} %copy.151, f32[2048,2]{1,0:T(8,128)} %copy.144), kind=kLoop, calls=%fused_computation.87 | loop fusion | flops 5500928 | bytes 12615680 | tf_op jit(solution)/shard_map/reduce_sum | solution.py:269
  816.0 290.8 %while.29 = (s32[]{:T(128)}, f32[2,1024,6,64]{1,0,3,2:T(2,128)}, f32[2,1024,6,64]{1,0,3,2:T(2,128)}, bf16[2,1024,6,64]{1,3,2,0:T(8,128)(2,1)}, f32[2,2,6]{2,1,0:...) while((s32[]{:T(128)}, f32[2,1024,6,64]{1,0,3,2:T(2,128)}, ...), condition=%wide.region_24.25_spmd, body=%wide.region_20.24_spmd.sunk | while | flops 4130072576 | bytes 286152160 | solution.py:284
  830.7 20.5 %multiply_reduce_fusion.14 = (f32[6,1024]{1,0:T(8,128)S(1)}, f32[6,1024,1024]{1,2,0:T(8,128)}) fusion(f32[6,1024,1024]{1,2,0:T(8,128)} %fusion.160, f32[6,1024]{1,0:T(8,128)S(1)} %dynamic-slice_bitcast_fusion.2, f32[6]{0:T(128)S(1)} %get-tuple-element.575, f32[6]{0:T(128)S(1)} %get-tuple-element.576, ...), kind=kOutput, calls=%fused_computation.38.clone.1 | convolution fusion | flops 849340416 | bytes 54051888 | tf_op jit(solution)/shard_map/while/body/eval_jaxpr/qhd,khd->hqk/dot_general | solution.py:80
  851.2 23.3 %fusion.161 = (f32[6]{0:T(128)S(1)}, f32[6]{0:T(128)S(1)}, bf16[6,1024,1024]{1,2,0:T(8,128)(2,1)}) fusion(pred[1024,1024]{0,1:T(8,128)(4,1)S(1)} %broadcast_compare_fusion.11, f32[6,1024,1024]{1,2,0:T(8,128)} %get-tuple-element.578, f32[6,1024,1024]{1,2,0:T(8,128)} %fusion.160, f32[6,1024]{1,0:T(8,128)S(1)} %get-tuple-element.579), kind=kLoop, calls=%fused_computation.35.clone.1 | loop fusion | flops 50331632 | bytes 63987760 | tf_op jit(solution)/shard_map/while/body/eval_jaxpr/reduce_sum | solution.py:117
  905.9 27.9 %dynamic_update_slice.37 = f32[2,1024,6,64]{1,0,3,2:T(2,128)} dynamic-update-slice(f32[2,1024,6,64]{1,0,3,2:T(2,128)} %get-tuple-element.630, f32[1,1024,6,64]{1,0,3,2:T(1,128)} %copy.205, s32[]{:T(128)S(6)} %copy.228, s32[]{:T(128)} %constant.51.clone.1..sunk, s32[]{:T(128)} %constant.51.clone.1..sunk, s32[]{:T(128)} %constant.51.clone.1..sunk) | dynamic-update-slice | bytes 3145732 | tf_op jit(solution)/shard_map/while/body/jit(dynamic_update_index_in_dim)/dynamic_update_slice | solution.py:284
  933.8 27.6 %dynamic_update_slice.36 = f32[2,1024,6,64]{1,0,3,2:T(2,128)} dynamic-update-slice(f32[2,1024,6,64]{1,0,3,2:T(2,128)} %get-tuple-element.629, f32[1,1024,6,64]{1,0,3,2:T(1,128)S(1)} %copy-done.1, s32[]{:T(128)S(6)} %copy.228, s32[]{:T(128)} %constant.51.clone.1..sunk, s32[]{:T(128)} %constant.51.clone.1..sunk, s32[]{:T(128)} %constant.51.clone.1..sunk) | dynamic-update-slice | bytes 3145732 | tf_op jit(solution)/shard_map/while/body/jit(dynamic_update_index_in_dim)/dynamic_update_slice | solution.py:284
  975.9 20.5 %multiply_reduce_fusion.14 = (f32[6,1024]{1,0:T(8,128)S(1)}, f32[6,1024,1024]{1,2,0:T(8,128)}) fusion(f32[6,1024,1024]{1,2,0:T(8,128)} %fusion.160, f32[6,1024]{1,0:T(8,128)S(1)} %dynamic-slice_bitcast_fusion.2, f32[6]{0:T(128)S(1)} %get-tuple-element.575, f32[6]{0:T(128)S(1)} %get-tuple-element.576, ...), kind=kOutput, calls=%fused_computation.38.clone.1 | convolution fusion | flops 849340416 | bytes 54051888 | tf_op jit(solution)/shard_map/while/body/eval_jaxpr/qhd,khd->hqk/dot_general | solution.py:80
  996.4 23.3 %fusion.161 = (f32[6]{0:T(128)S(1)}, f32[6]{0:T(128)S(1)}, bf16[6,1024,1024]{1,2,0:T(8,128)(2,1)}) fusion(pred[1024,1024]{0,1:T(8,128)(4,1)S(1)} %broadcast_compare_fusion.11, f32[6,1024,1024]{1,2,0:T(8,128)} %get-tuple-element.578, f32[6,1024,1024]{1,2,0:T(8,128)} %fusion.160, f32[6,1024]{1,0:T(8,128)S(1)} %get-tuple-element.579), kind=kLoop, calls=%fused_computation.35.clone.1 | loop fusion | flops 50331632 | bytes 63987760 | tf_op jit(solution)/shard_map/while/body/eval_jaxpr/reduce_sum | solution.py:117
  1051.1 27.9 %dynamic_update_slice.37 = f32[2,1024,6,64]{1,0,3,2:T(2,128)} dynamic-update-slice(f32[2,1024,6,64]{1,0,3,2:T(2,128)} %get-tuple-element.630, f32[1,1024,6,64]{1,0,3,2:T(1,128)} %copy.205, s32[]{:T(128)S(6)} %copy.228, s32[]{:T(128)} %constant.51.clone.1..sunk, s32[]{:T(128)} %constant.51.clone.1..sunk, s32[]{:T(128)} %constant.51.clone.1..sunk) | dynamic-update-slice | bytes 3145732 | tf_op jit(solution)/shard_map/while/body/jit(dynamic_update_index_in_dim)/dynamic_update_slice | solution.py:284
  1079.0 27.6 %dynamic_update_slice.36 = f32[2,1024,6,64]{1,0,3,2:T(2,128)} dynamic-update-slice(f32[2,1024,6,64]{1,0,3,2:T(2,128)} %get-tuple-element.629, f32[1,1024,6,64]{1,0,3,2:T(1,128)S(1)} %copy-done.1, s32[]{:T(128)S(6)} %copy.228, s32[]{:T(128)} %constant.51.clone.1..sunk, s32[]{:T(128)} %constant.51.clone.1..sunk, s32[]{:T(128)} %constant.51.clone.1..sunk) | dynamic-update-slice | bytes 3145732 | tf_op jit(solution)/shard_map/while/body/jit(dynamic_update_index_in_dim)/dynamic_update_slice | solution.py:284
  1169.6 126.0 %all-reduce.7.cloned.1.call-done = f32[592896]{0:T(1024)} async-done(((f32[592896]{0:T(1024)}), f32[592896]{0:T(1024)}) %all-reduce.7.cloned.1.call-update) | async-done | bytes 2371600
  (387 shorter events, 523.1 us)
Async XLA Ops:
  7.2 139.7 %all-reduce.5.cloned.1.call-start = ((), (), s32[]{:S(2)}) async-start(), calls=%async_computation.8 | async-start | bytes 2371584
  12.9 38.2 %copy-start.28 = (bf16[2048,384]{1,0:T(8,128)(2,1)S(1)}, bf16[2048,384]{1,0:T(8,128)(2,1)}, u32[]{:S(2)}) copy-start(bf16[2048,384]{1,0:T(8,128)(2,1)} %param.15) | copy-start | bytes 4718596
  19.1 31.4 %copy-start.66 = (s32[4096,1]{0,1:T(1,128)}, s32[4096,1]{0,1:T(1,128)S(1)}, u32[]{:S(2)}) copy-start(s32[4096,1]{0,1:T(1,128)S(1)} %compare_select_fusion) | copy-start | bytes 49156
  51.9 97.3 %copy-start.4 = (bf16[2048,384]{0,1:T(8,128)(2,1)}, bf16[2048,384]{0,1:T(8,128)(2,1)S(1)}, u32[]{:S(2)}) copy-start(bf16[2048,384]{0,1:T(8,128)(2,1)S(1)} %copy.139) | copy-start | bytes 4718596
  53.0 96.2 %copy-start.56 = (f32[2048]{0:T(1024)}, f32[2048]{0:T(1024)S(1)}, u32[]{:S(2)}) copy-start(f32[2048]{0:T(1024)S(1)} %get-tuple-element.408) | copy-start | bytes 24580
  74.0 77.9 %copy-start.68 = (f32[384]{0:T(512)}, f32[384]{0:T(512)S(1)}, u32[]{:S(2)}) copy-start(f32[384]{0:T(512)S(1)} %get-tuple-element.305) | copy-start | bytes 4612
  284.6 34.9 %copy-start.58 = (s32[8192]{0:T(1024)S(1)}, s32[8192]{0:T(1024)}, u32[]{:S(2)}) copy-start(s32[8192]{0:T(1024)} %get-tuple-element.403) | copy-start | bytes 98308
  319.6 33.3 %copy-start.74 = (pred[8,1024]{1,0:T(8,128)(4,1)S(1)}, pred[8,1024]{1,0:T(8,128)(4,1)}, u32[]{:S(2)}) copy-start(pred[8,1024]{1,0:T(8,128)(4,1)} %broadcast_in_dim.212) | copy-start | bytes 24580
  436.8 76.4 %all-to-all-start.2 = ((bf16[8,1024,384]{2,1,0:T(8,128)(2,1)}), bf16[8,1024,384]{2,1,0:T(8,128)(2,1)}, u32[]{:S(2)}, u32[]{:S(2)}) async-start(bf16[8,1024,384]{2,1,0:T(8,128)(2,1)} %get-tuple-element.411), calls=%async_computation.2 | async-start | bytes 12582912 | tf_op jit(solution)/shard_map/all_to_all | solution.py:131
  458.6 29.7 %slice-start = ((s8[6291456]{0:T(1024)(128)(4,1)}), s8[4194304]{0:T(1024)(128)(4,1)S(1)}, s32[]{:S(2)}) async-start(s8[6291456]{0:T(1024)(128)(4,1)} %bitcast.320), calls=%async_computation.10 | async-start | bytes 8388608
  557.2 76.4 %all-to-all-start.3 = ((bf16[8,1024,384]{2,1,0:T(8,128)(2,1)}), bf16[8,1024,384]{2,1,0:T(8,128)(2,1)}, u32[]{:S(2)}, u32[]{:S(2)}) async-start(bf16[8,1024,384]{2,1,0:T(8,128)(2,1)} %bitcast.323), calls=%async_computation.3 | async-start | bytes 12582912 | tf_op jit(solution)/shard_map/all_to_all | solution.py:135
  562.0 95.2 %reduce-scatter.5.cloned.1.call-start = ((), (), s32[]{:S(2)}) async-start(), calls=%async_computation.7 | async-start | bytes 983040 | tf_op jit(solution)/shard_map/reduce_scatter | solution.py:163
  633.6 114.5 %all-to-all-start.1 = ((bf16[8,1024,384]{2,1,0:T(8,128)(2,1)}), bf16[8,1024,384]{2,1,0:T(8,128)(2,1)}, u32[]{:S(2)}, u32[]{:S(2)}) async-start(bf16[8,1024,384]{2,1,0:T(8,128)(2,1)} %bitcast.330), calls=%async_computation.1 | async-start | bytes 12582912 | tf_op jit(solution)/shard_map/all_to_all | solution.py:135
  638.6 53.9 %reduce-scatter.3.cloned.1.call-start = ((), (), s32[]{:S(2)}) async-start(), calls=%async_computation.6 | async-start | bytes 1966080 | tf_op jit(solution)/shard_map/reduce_scatter | solution.py:162
  655.6 37.0 %copy-start.27 = (f32[4,1,2,384,128]{4,3,2,1,0:T(8,128)S(1)}, f32[4,1,2,384,128]{4,3,2,1,0:T(8,128)}, u32[]{:S(2)}) copy-start(f32[4,1,2,384,128]{4,3,2,1,0:T(8,128)} %param.23) | copy-start | bytes 4718596
  655.6 640.1 %all-reduce.7.cloned.1.call-start = ((), (), s32[]{:S(2)}) async-start(), calls=%async_computation.9 | async-start | bytes 4743168
  770.4 24.2 %copy-start.3 = (f32[2048,384]{0,1:T(8,128)S(1)}, f32[2048,384]{0,1:T(8,128)}, u32[]{:S(2)}) copy-start(f32[2048,384]{0,1:T(8,128)} %copy-done.2) | copy-start | bytes 9437188
  770.4 24.2 %copy-start.63 = (f32[2048]{0:T(1024)S(1)}, f32[2048]{0:T(1024)}, u32[]{:S(2)}) copy-start(f32[2048]{0:T(1024)} %copy-done.62) | copy-start | bytes 24580
  905.9 27.9 %copy-start.1 = (f32[1,1024,6,64]{1,0,3,2:T(1,128)S(1)}, f32[1,1024,6,64]{1,0,3,2:T(1,128)}, u32[]{:S(2)}) copy-start(f32[1,1024,6,64]{1,0,3,2:T(1,128)} %copy.204) | copy-start | bytes 4718596 | tf_op jit(solution)/shard_map/while
  1051.1 27.9 %copy-start.1 = (f32[1,1024,6,64]{1,0,3,2:T(1,128)S(1)}, f32[1,1024,6,64]{1,0,3,2:T(1,128)}, u32[]{:S(2)}) copy-start(f32[1,1024,6,64]{1,0,3,2:T(1,128)} %copy.204) | copy-start | bytes 4718596 | tf_op jit(solution)/shard_map/while
  1167.4 128.3 %copy-start.38 = (f32[18528]{0:T(1024)S(1)}, f32[18528]{0:T(1024)}, u32[]{:S(2)}) copy-start(f32[18528]{0:T(1024)} %copy-done.37) | copy-start | bytes 222340
  1167.4 128.3 %copy-start.44 = (f32[18528]{0:T(1024)S(1)}, f32[18528]{0:T(1024)}, u32[]{:S(2)}) copy-start(f32[18528]{0:T(1024)} %get-tuple-element.296) | copy-start | bytes 222340
  1167.4 128.2 %copy-start.45 = (f32[18528]{0:T(1024)S(1)}, f32[18528]{0:T(1024)}, u32[]{:S(2)}) copy-start(f32[18528]{0:T(1024)} %get-tuple-element.297) | copy-start | bytes 222340
  1167.4 129.9 %copy-start.43 = (f32[18528]{0:T(1024)S(1)}, f32[18528]{0:T(1024)}, u32[]{:S(2)}) copy-start(f32[18528]{0:T(1024)} %get-tuple-element.299) | copy-start | bytes 222340
  (75 other events, 448.4 us)
Sparse Core Ops, SparseCore 0:
  14.0 132.8 all-reduce.4
  572.7 24.7 reduce-scatter.4
  655.7 36.7 reduce-scatter.2
  1163.5 132.1 all-reduce.6
